TPU v7x, 512 devices: a whole 4x4x16 slice. The times are simulated.
512 devices in a mesh: dp: 32 (over z, core), seq: 16 (over y, x).
Axes of the slice: x: 4, y: 4, z: 16, core: 2. Of those that a mesh axis runs over, the one named last changes fastest.
Arguments:
- q_pre: bfloat16 [32, 2048, 16, 128], P('dp', 'seq'), may hold values from -6 to 6
- k_pre: bfloat16 [32, 2048, 8, 128], P('dp', 'seq'), may hold values from -6 to 6
- values: bfloat16 [32, 2048, 8, 128], P('dp', 'seq'), may hold values from -6 to 6
- grad_out: bfloat16 [32, 2048, 16, 128], P('dp', 'seq'), may hold values from -6 to 6
- segment_ids: int32 [32, 2048], P('dp', 'seq'), may hold values from 0 to 7, never falling along the last dimension, each value on 1 to 1024 neighbouring positions
- q_gain: float32 [128], replicated, may hold values from 0.1 to 1.9
- k_gain: float32 [128], replicated, may hold values from 0.1 to 1.9
Outputs:
- grad_q: bfloat16 [32, 2048, 16, 128], P('dp', 'seq')
- grad_k: bfloat16 [32, 2048, 8, 128], P('dp', 'seq')
- grad_v: bfloat16 [32, 2048, 8, 128], P('dp', 'seq')
- grad_q_gain: float32 [128], replicated
- grad_k_gain: float32 [128], replicated
Inputs may be any that keep to these rules, and one draw needn't show every extreme that they name: `segment_ids`: along a span the ids never fall, and each id from 0 to 7 names one run of consecutive tokens.
All inputs are finite; a program needn't handle non-finite values.
Results may differ from a plain program's by a relative error of at most 0.017.
Values may be sent and summed in bfloat16 or wider, within the bound.
A program may use at most 64 MiB of HBM per device.

v0:
```python
import jax
import jax.numpy as jnp
from jax import lax
from jax.sharding import PartitionSpec as P

PRESCALE = 168
DOCS = 8
norm_epsilon = 1e-06
rope_base = 1000000.0
rope_factor = 8.0


def document_positions(segments, docs):
    labels = jnp.arange(docs, dtype=jnp.int32)
    member = (segments[:, None] == labels[None, :]).astype(jnp.int32)
    counts = jnp.sum(member, axis=0)
    starts = jnp.cumsum(counts) - counts
    first = jnp.sum(member * starts[None, :], axis=1)
    return (jnp.arange(segments.shape[0], dtype=jnp.int32) - first, first)


def embed(rows, gain, positions):
    width = rows.shape[-1]
    half = width // 2
    scale = lax.rsqrt(jnp.mean(rows * rows, axis=-1, keepdims=True) + norm_epsilon)
    normed = rows * scale * gain
    freqs = rope_base ** (-(jnp.arange(half, dtype=jnp.float32) * 2.0 / width))
    angles = (positions.astype(jnp.float32) / rope_factor)[:, None] * freqs[None, :]
    cosine = jnp.cos(angles)[:, None, :]
    sine = jnp.sin(angles)[:, None, :]
    first_half = normed[..., :half]
    second_half = normed[..., half:]
    return jnp.concatenate(
        [first_half * cosine - second_half * sine, second_half * cosine + first_half * sine],
        axis=-1,
    )


def attend_blocks(queries, keys, vals, upstream, segments):
    total = queries.shape[0]
    group = queries.shape[1]
    width = queries.shape[2]
    block = min(512, total)
    count = total // block
    rows = block * group
    score_scale = float(PRESCALE) ** (-0.5)
    contract_last = (((1,), (1,)), ((), ()))
    contract_first = (((0,), (0,)), ((), ()))

    def query_block(query_index, carry):
        query_grads, key_grads, value_grads = carry
        start = query_index * block
        query_rows = lax.dynamic_slice_in_dim(queries, start, block, 0).reshape(rows, width)
        upstream_rows = lax.dynamic_slice_in_dim(upstream, start, block, 0).reshape(rows, width)
        query_segs = jnp.repeat(lax.dynamic_slice_in_dim(segments, start, block, 0), group)
        query_places = jnp.repeat(start + jnp.arange(block, dtype=jnp.int32), group)
        lower = 0

        def key_scores(key_index):
            key_start = key_index * block
            key_rows = lax.dynamic_slice_in_dim(keys, key_start, block, 0)
            value_rows = lax.dynamic_slice_in_dim(vals, key_start, block, 0)
            key_segs = lax.dynamic_slice_in_dim(segments, key_start, block, 0)
            key_places = key_start + jnp.arange(block, dtype=jnp.int32)
            scores = score_scale * lax.dot_general(
                query_rows, key_rows, contract_last, preferred_element_type=jnp.float32
            )
            visible = (query_segs[:, None] == key_segs[None, :]) & (
                query_places[:, None] >= key_places[None, :]
            )
            return (scores, visible, key_rows, value_rows, key_start)

        def forward_step(key_index, state):
            totals, numer = state
            scores, visible, key_rows, value_rows, key_start = key_scores(key_index)
            raw = jnp.where(visible, jnp.exp(scores), 0.0)
            numer = numer + jnp.dot(
                raw.astype(jnp.bfloat16), value_rows, preferred_element_type=jnp.float32
            )
            return (totals + jnp.sum(raw, axis=1), numer)

        totals, numer = lax.fori_loop(
            lower,
            query_index + 1,
            forward_step,
            (jnp.zeros((rows,), jnp.float32), jnp.zeros((rows, width), jnp.float32)),
        )
        outputs = numer / totals[:, None]
        delta = jnp.sum(upstream_rows.astype(jnp.float32) * outputs, axis=1)
        logsum = jnp.log(totals)

        def backward_step(key_index, state):
            query_part, key_acc, value_acc = state
            scores, visible, key_rows, value_rows, key_start = key_scores(key_index)
            probs = jnp.where(visible, jnp.exp(scores - logsum[:, None]), 0.0).astype(jnp.bfloat16)
            prob_grads = lax.dot_general(
                upstream_rows, value_rows, contract_last, preferred_element_type=jnp.float32
            )
            score_grads = (
                probs.astype(jnp.float32) * (prob_grads - delta[:, None]) * score_scale
            ).astype(jnp.bfloat16)
            query_part = query_part + jnp.dot(
                score_grads, key_rows, preferred_element_type=jnp.float32
            )
            key_part = lax.dot_general(
                score_grads, query_rows, contract_first, preferred_element_type=jnp.float32
            )
            value_part = lax.dot_general(
                probs, upstream_rows, contract_first, preferred_element_type=jnp.float32
            )
            key_acc = lax.dynamic_update_slice_in_dim(
                key_acc,
                lax.dynamic_slice_in_dim(key_acc, key_start, block, 0) + key_part,
                key_start,
                0,
            )
            value_acc = lax.dynamic_update_slice_in_dim(
                value_acc,
                lax.dynamic_slice_in_dim(value_acc, key_start, block, 0) + value_part,
                key_start,
                0,
            )
            return (query_part, key_acc, value_acc)

        query_part, key_grads, value_grads = lax.fori_loop(
            lower,
            query_index + 1,
            backward_step,
            (jnp.zeros((rows, width), jnp.float32), key_grads, value_grads),
        )
        query_grads = lax.dynamic_update_slice_in_dim(query_grads, query_part, start * group, 0)
        return (query_grads, key_grads, value_grads)

    initial = (
        jnp.zeros((total * group, width), jnp.float32),
        jnp.zeros((total, width), jnp.float32),
        jnp.zeros((total, width), jnp.float32),
    )
    query_grads, key_grads, value_grads = lax.fori_loop(0, count, query_block, initial)
    return (query_grads.reshape(total, group, width), key_grads, value_grads)


def body(q_pre, k_pre, values, grad_out, segment_ids, q_gain, k_gain):
    segments = lax.all_gather(segment_ids, "seq", axis=1, tiled=True)[0]
    positions, first = document_positions(segments, DOCS)
    local = q_pre.shape[1]
    heads = q_pre.shape[2]
    kv_heads = k_pre.shape[2]
    width = q_pre.shape[3]
    group = heads // kv_heads

    def embed_rows(rows, gain):
        return embed(rows, gain, positions)

    key_copies = jnp.repeat(k_pre[0], group, axis=1)
    value_copies = jnp.repeat(values[0], group, axis=1)
    query_here, upstream_here, key_here, value_here = (
        lax.all_to_all(q_pre[0], "seq", split_axis=1, concat_axis=0, tiled=True),
        lax.all_to_all(grad_out[0], "seq", split_axis=1, concat_axis=0, tiled=True),
        lax.all_to_all(key_copies, "seq", split_axis=1, concat_axis=0, tiled=True),
        lax.all_to_all(value_copies, "seq", split_axis=1, concat_axis=0, tiled=True),
    )
    query_rot, query_back = jax.vjp(embed_rows, query_here.astype(jnp.float32), q_gain)
    key_rot, key_back = jax.vjp(embed_rows, key_here.astype(jnp.float32), k_gain)
    query_hat = query_rot.astype(jnp.bfloat16)
    key_hat = key_rot.astype(jnp.bfloat16)
    query_list, key_list, value_list = ([], [], [])
    query_part, key_part, value_part = attend_blocks(
        query_hat, key_hat[:, 0], value_here[:, 0], upstream_here, segments
    )
    query_list.append(query_part)
    key_list.append(key_part)
    value_list.append(value_part)
    query_input, query_gain_part = query_back(query_list[0])
    key_input, key_gain_part = key_back(jnp.stack(key_list, axis=1))
    value_input = jnp.stack(value_list, axis=1)
    query_return, key_return, value_return = (
        lax.all_to_all(
            query_input.astype(jnp.bfloat16), "seq", split_axis=0, concat_axis=1, tiled=True
        ).astype(query_input.dtype),
        lax.all_to_all(
            key_input.astype(jnp.bfloat16), "seq", split_axis=0, concat_axis=1, tiled=True
        ).astype(key_input.dtype),
        lax.all_to_all(
            value_input.astype(jnp.bfloat16), "seq", split_axis=0, concat_axis=1, tiled=True
        ).astype(value_input.dtype),
    )
    grad_q = query_return.astype(jnp.bfloat16)
    grad_k = jnp.sum(key_return.reshape(local, kv_heads, group, width), axis=2).astype(jnp.bfloat16)
    grad_v = jnp.sum(value_return.reshape(local, kv_heads, group, width), axis=2).astype(
        jnp.bfloat16
    )
    gain_totals = lax.psum((query_gain_part, key_gain_part), ("dp", "seq"))
    return (grad_q[None], grad_k[None], grad_v[None], gain_totals[0], gain_totals[1])


def solution(mesh):
    return jax.shard_map(
        body,
        mesh=mesh,
        in_specs=(
            P("dp", "seq", None, None),
            P("dp", "seq", None, None),
            P("dp", "seq", None, None),
            P("dp", "seq", None, None),
            P("dp", "seq"),
            P(),
            P(),
        ),
        out_specs=(
            P("dp", "seq", None, None),
            P("dp", "seq", None, None),
            P("dp", "seq", None, None),
            P(),
            P(),
        ),
        check_vma=False,
    )
```

profile of v0, /device:TPU:1, one launch (start us, length us, event | category | flops | bytes accessed | tf_op | source)
XLA Modules:
  0.0 308.5 jit_solution(509402824562934716)
XLA Ops:
  0.6 2.0 copy.172
  2.6 7.7 %all-to-all-start = ((bf16[128,16,128]{2,0,1:T(8,128)(2,1)}), bf16[128,16,128]{2,0,1:T(8,128)(2,1)S(1)}, u32[]{:S(2)}, u32[]{:S(2)}) async-start(bf16[128,16,128]{2,0,1:T(8,128)(2,1)} %bitcast.130), calls=%async_computation | async-start | bytes 1048576 | tf_op jit(solution)/shard_map/all_to_all | solution.py:158
  10.4 17.6 %all_gather.3 = s32[1,2048]{1,0:T(1,128)S(1)} all-gather(s32[1,128]{1,0:T(1,128)S(1)} %copy-done.13), channel_id=1, replica_groups=mesh['dp'=32,'seq'=16] {'seq'}, dimensions={1}, use_global_device_ids=true | all-gather | bytes 8704 | tf_op jit(solution)/shard_map/all_gather | solution.py:144
  31.3 4.0 %all-to-all-start.1 = ((bf16[128,16,128]{0,2,1:T(8,128)(2,1)}), bf16[128,16,128]{0,2,1:T(8,128)(2,1)S(1)}, u32[]{:S(2)}, u32[]{:S(2)}) async-start(bf16[128,16,128]{0,2,1:T(8,128)(2,1)} %bitcast.12), calls=%async_computation.1 | async-start | bytes 1048576 | tf_op jit(solution)/shard_map/all_to_all | solution.py:160
  37.4 6.9 %all-to-all-done.1 = bf16[128,16,128]{0,2,1:T(8,128)(2,1)S(1)} async-done(((bf16[128,16,128]{0,2,1:T(8,128)(2,1)}), bf16[128,16,128]{0,2,1:T(8,128)(2,1)S(1)}, u32[]{:S(2)}, u32[]{:S(2)}) %all-to-all-start.1) | async-done | bytes 524320 | tf_op jit(solution)/shard_map/all_to_all | solution.py:160
  45.3 3.6 %all-to-all-start.2 = ((bf16[128,16,128]{2,0,1:T(8,128)(2,1)}), bf16[128,16,128]{2,0,1:T(8,128)(2,1)S(1)}, u32[]{:S(2)}, u32[]{:S(2)}) async-start(bf16[128,16,128]{2,0,1:T(8,128)(2,1)} %bitcast.20), calls=%async_computation.2 | async-start | bytes 1048576 | tf_op jit(solution)/shard_map/all_to_all | solution.py:161
  50.8 7.0 %all-to-all-done.2 = bf16[128,16,128]{2,0,1:T(8,128)(2,1)S(1)} async-done(((bf16[128,16,128]{2,0,1:T(8,128)(2,1)}), bf16[128,16,128]{2,0,1:T(8,128)(2,1)S(1)}, u32[]{:S(2)}, u32[]{:S(2)}) %all-to-all-start.2) | async-done | bytes 524320 | tf_op jit(solution)/shard_map/all_to_all | solution.py:161
  57.8 4.2 %all-to-all-start.3 = ((bf16[128,16,128]{2,0,1:T(8,128)(2,1)}), bf16[128,16,128]{2,0,1:T(8,128)(2,1)}, u32[]{:S(2)}, u32[]{:S(2)}) async-start(bf16[128,16,128]{2,0,1:T(8,128)(2,1)} %bitcast.129), calls=%async_computation.3 | async-start | bytes 1048576 | tf_op jit(solution)/shard_map/all_to_all | solution.py:159
  62.1 3.1 fusion.63
  66.2 4.8 %all-to-all-done.3 = bf16[128,16,128]{2,0,1:T(8,128)(2,1)} async-done(((bf16[128,16,128]{2,0,1:T(8,128)(2,1)}), bf16[128,16,128]{2,0,1:T(8,128)(2,1)}, u32[]{:S(2)}, u32[]{:S(2)}) %all-to-all-start.3) | async-done | bytes 524320 | tf_op jit(solution)/shard_map/all_to_all | solution.py:159
  72.3 69.1 %while.79 = (s32[]{:T(128)}, f32[2048,128]{0,1:T(8,128)}, f32[2048,128]{1,0:T(8,128)S(1)}, f32[2048,128]{1,0:T(8,128)S(1)}, bf16[2048,1,128]{0,2,1:T(8,128)(2,1)...) while((s32[]{:T(128)}, f32[2048,128]{0,1:T(8,128)}, ...), condition=%wide.region_12.13_spmd, body=%wide.region_5.12_spmd.sunk | while | flops 475268608 | bytes 14478353 | solution.py:139
  73.2 1.9 while.80
  73.3 1.4 fusion.101
  76.3 3.7 %while.81 = (s32[]{:T(128)}, f32[512,128]{1,0:T(8,128)S(1)}, f32[2048,128]{1,0:T(8,128)S(1)}, f32[2048,128]{1,0:T(8,128)S(1)}, s32[]{:T(128)}, /*index=5*/s32[51...) while((s32[]{:T(128)}, f32[512,128]{1,0:T(8,128)S(1)}, ...), condition=%wide.region_11.11_spmd.clone, body=%wide.region_10.10_spmd.clone.sunk | while | flops 338887680 | bytes 5656819 | solution.py:125
  82.1 3.7 %while.80 = (s32[]{:T(128)}, f32[512]{0:T(512)S(1)}, f32[512,128]{1,0:T(8,128)S(1)}, s32[]{:T(128)}, s32[512]{0:T(512)S(1)}, /*index=5*/s32[2048]{0:T(1024)S(1)}...) while((s32[]{:T(128)}, f32[512]{0:T(512)S(1)}, ...), condition=%wide.region_8.8_spmd.clone, body=%wide.region_6.7_spmd.clone.sunk | while | flops 136119296 | bytes 1990855 | solution.py:82
  82.2 1.4 fusion.101
  84.1 1.4 fusion.101
  87.0 7.4 %while.81 = (s32[]{:T(128)}, f32[512,128]{1,0:T(8,128)S(1)}, f32[2048,128]{1,0:T(8,128)S(1)}, f32[2048,128]{1,0:T(8,128)S(1)}, s32[]{:T(128)}, /*index=5*/s32[51...) while((s32[]{:T(128)}, f32[512,128]{1,0:T(8,128)S(1)}, ...), condition=%wide.region_11.11_spmd.clone, body=%wide.region_10.10_spmd.clone.sunk | while | flops 338887680 | bytes 5656819 | solution.py:125
  96.6 5.6 %while.80 = (s32[]{:T(128)}, f32[512]{0:T(512)S(1)}, f32[512,128]{1,0:T(8,128)S(1)}, s32[]{:T(128)}, s32[512]{0:T(512)S(1)}, /*index=5*/s32[2048]{0:T(1024)S(1)}...) while((s32[]{:T(128)}, f32[512]{0:T(512)S(1)}, ...), condition=%wide.region_8.8_spmd.clone, body=%wide.region_6.7_spmd.clone.sunk | while | flops 136119296 | bytes 1990855 | solution.py:82
  98.6 1.4 fusion.101
  103.4 11.1 %while.81 = (s32[]{:T(128)}, f32[512,128]{1,0:T(8,128)S(1)}, f32[2048,128]{1,0:T(8,128)S(1)}, f32[2048,128]{1,0:T(8,128)S(1)}, s32[]{:T(128)}, /*index=5*/s32[51...) while((s32[]{:T(128)}, f32[512,128]{1,0:T(8,128)S(1)}, ...), condition=%wide.region_11.11_spmd.clone, body=%wide.region_10.10_spmd.clone.sunk | while | flops 338887680 | bytes 5656819 | solution.py:125
  116.6 7.5 %while.80 = (s32[]{:T(128)}, f32[512]{0:T(512)S(1)}, f32[512,128]{1,0:T(8,128)S(1)}, s32[]{:T(128)}, s32[512]{0:T(512)S(1)}, /*index=5*/s32[2048]{0:T(1024)S(1)}...) while((s32[]{:T(128)}, f32[512]{0:T(512)S(1)}, ...), condition=%wide.region_8.8_spmd.clone, body=%wide.region_6.7_spmd.clone.sunk | while | flops 136119296 | bytes 1990855 | solution.py:82
  116.7 1.4 fusion.101
  118.6 1.4 fusion.101
  125.3 14.8 %while.81 = (s32[]{:T(128)}, f32[512,128]{1,0:T(8,128)S(1)}, f32[2048,128]{1,0:T(8,128)S(1)}, f32[2048,128]{1,0:T(8,128)S(1)}, s32[]{:T(128)}, /*index=5*/s32[51...) while((s32[]{:T(128)}, f32[512,128]{1,0:T(8,128)S(1)}, ...), condition=%wide.region_11.11_spmd.clone, body=%wide.region_10.10_spmd.clone.sunk | while | flops 338887680 | bytes 5656819 | solution.py:125
  142.7 4.1 %fusion.60 = (f32[2048,1,64]{0,2,1:T(8,128)S(1)}, f32[2048,1,64]{0,2,1:T(8,128)S(1)}, f32[2048,1,64]{0,2,1:T(8,128)S(1)}, f32[2048,1,64]{0,2,1:T(8,128)S(1)}) fusion(f32[2048,1,128]{0,2,1:T(8,128)} %bitcast.158, f32[64]{0:T(128)S(1)} %negate_power_fusion, f32[2048]{0:T(1024)S(1)} %convert_multiply_fusion.1, f32[2048,1,128]{0,2,1:T(8,128)} %bitcast.157), kind=kLoop, calls=%fused_computation.89 | loop fusion | flops 1966080 | bytes 4202752 | tf_op jit(solution)/shard_map/transpose(jvp())/add_any | solution.py:34
  151.6 3.6 %all-to-all-start.4 = ((bf16[16,2,8192]{2,1,0:T(2,128)(2,1)}), bf16[16,2,8192]{2,1,0:T(2,128)(2,1)S(1)}, u32[]{:S(2)}, u32[]{:S(2)}) async-start(bf16[16,2,8192]{2,1,0:T(2,128)(2,1)} %reshape.576), calls=%async_computation.4 | async-start | bytes 1048576 | tf_op jit(solution)/shard_map/all_to_all | solution.py:178
  157.4 6.8 %all-to-all-done.4 = bf16[16,2,8192]{2,1,0:T(2,128)(2,1)S(1)} async-done(((bf16[16,2,8192]{2,1,0:T(2,128)(2,1)}), bf16[16,2,8192]{2,1,0:T(2,128)(2,1)S(1)}, u32[]{:S(2)}, u32[]{:S(2)}) %all-to-all-start.4) | async-done | bytes 524320 | tf_op jit(solution)/shard_map/all_to_all | solution.py:178
  164.1 3.6 %all-to-all-start.5 = ((bf16[16,2,8192]{2,1,0:T(2,128)(2,1)}), bf16[16,2,8192]{2,1,0:T(2,128)(2,1)S(1)}, u32[]{:S(2)}, u32[]{:S(2)}) async-start(bf16[16,2,8192]{2,1,0:T(2,128)(2,1)} %reshape.578), calls=%async_computation.5 | async-start | bytes 1048576 | tf_op jit(solution)/shard_map/all_to_all | solution.py:181
  169.7 9.0 %all-to-all-done.5 = bf16[16,2,8192]{2,1,0:T(2,128)(2,1)S(1)} async-done(((bf16[16,2,8192]{2,1,0:T(2,128)(2,1)}), bf16[16,2,8192]{2,1,0:T(2,128)(2,1)S(1)}, u32[]{:S(2)}, u32[]{:S(2)}) %all-to-all-start.5) | async-done | bytes 524320 | tf_op jit(solution)/shard_map/all_to_all | solution.py:181
  178.7 3.6 %all-to-all-start.6 = ((bf16[16,2,8192]{2,1,0:T(2,128)(2,1)}), bf16[16,2,8192]{2,1,0:T(2,128)(2,1)S(1)}, u32[]{:S(2)}, u32[]{:S(2)}) async-start(bf16[16,2,8192]{2,1,0:T(2,128)(2,1)} %reshape.580), calls=%async_computation.6 | async-start | bytes 1048576 | tf_op jit(solution)/shard_map/all_to_all | solution.py:184
  182.3 121.2 %all-reduce.4 = (f32[128]{0:T(128)}, f32[128]{0:T(128)}) all-reduce(f32[128]{0:T(128)S(1)} %get-tuple-element.430, f32[128]{0:T(128)S(1)} %get-tuple-element.428), channel_id=1, replica_groups=mesh['dp'=32,'seq'=16] {'dp','seq'}, use_global_device_ids=true, to_apply=%region_18.19 | all-reduce | flops 256 | bytes 2048 | tf_op jit(solution)/shard_map/psum | solution.py:193
  (248 shorter events, 85.4 us)
Async XLA Ops:
  2.6 7.7 %copy-start.13 = (s32[1,128]{1,0:T(1,128)S(1)}, s32[1,128]{1,0:T(1,128)}, u32[]{:S(2)}) copy-start(s32[1,128]{1,0:T(1,128)} %param.17) | copy-start | bytes 1540
  2.6 25.7 %copy-start.9 = (bf16[1,128,8,128]{3,2,1,0:T(8,128)(2,1)S(1)}, bf16[1,128,8,128]{3,2,1,0:T(8,128)(2,1)}, u32[]{:S(2)}) copy-start(bf16[1,128,8,128]{3,2,1,0:T(8,128)(2,1)} %param.14) | copy-start | bytes 786436
  2.6 27.8 %all-to-all-start = ((bf16[128,16,128]{2,0,1:T(8,128)(2,1)}), bf16[128,16,128]{2,0,1:T(8,128)(2,1)S(1)}, u32[]{:S(2)}, u32[]{:S(2)}) async-start(bf16[128,16,128]{2,0,1:T(8,128)(2,1)} %bitcast.130), calls=%async_computation | async-start | bytes 1048576 | tf_op jit(solution)/shard_map/all_to_all | solution.py:158
  10.3 18.2 %copy-start.10 = (bf16[1,128,8,128]{3,2,1,0:T(8,128)(2,1)S(1)}, bf16[1,128,8,128]{3,2,1,0:T(8,128)(2,1)}, u32[]{:S(2)}) copy-start(bf16[1,128,8,128]{3,2,1,0:T(8,128)(2,1)} %param.15) | copy-start | bytes 786436
  28.3 1.0 copy-start.8
  31.3 13.0 %all-to-all-start.1 = ((bf16[128,16,128]{0,2,1:T(8,128)(2,1)}), bf16[128,16,128]{0,2,1:T(8,128)(2,1)S(1)}, u32[]{:S(2)}, u32[]{:S(2)}) async-start(bf16[128,16,128]{0,2,1:T(8,128)(2,1)} %bitcast.12), calls=%async_computation.1 | async-start | bytes 1048576 | tf_op jit(solution)/shard_map/all_to_all | solution.py:160
  35.8 0.7 copy-start.12
  36.5 1.0 copy-start
  44.3 4.7 %copy-start.2 = (bf16[128,16,128]{0,2,1:T(8,128)(2,1)}, bf16[128,16,128]{0,2,1:T(8,128)(2,1)S(1)}, u32[]{:S(2)}) copy-start(bf16[128,16,128]{0,2,1:T(8,128)(2,1)S(1)} %all-to-all-done.1) | copy-start | bytes 1572868
  45.3 12.5 %all-to-all-start.2 = ((bf16[128,16,128]{2,0,1:T(8,128)(2,1)}), bf16[128,16,128]{2,0,1:T(8,128)(2,1)S(1)}, u32[]{:S(2)}, u32[]{:S(2)}) async-start(bf16[128,16,128]{2,0,1:T(8,128)(2,1)} %bitcast.20), calls=%async_computation.2 | async-start | bytes 1048576 | tf_op jit(solution)/shard_map/all_to_all | solution.py:161
  49.0 0.7 copy-start.11
  50.8 11.2 %copy-start.4 = (f32[2048,1,128]{0,2,1:T(8,128)S(1)}, f32[2048,1,128]{0,2,1:T(8,128)}, u32[]{:S(2)}) copy-start(f32[2048,1,128]{0,2,1:T(8,128)} %fusion.33) | copy-start | bytes 3145732
  57.8 13.2 %all-to-all-start.3 = ((bf16[128,16,128]{2,0,1:T(8,128)(2,1)}), bf16[128,16,128]{2,0,1:T(8,128)(2,1)}, u32[]{:S(2)}, u32[]{:S(2)}) async-start(bf16[128,16,128]{2,0,1:T(8,128)(2,1)} %bitcast.129), calls=%async_computation.3 | async-start | bytes 1048576 | tf_op jit(solution)/shard_map/all_to_all | solution.py:159
  65.2 1.0 copy-start.7
  72.4 0.8 copy-start.5
  80.1 1.1 copy-start.6
  81.3 0.8 copy-start.5
  94.6 1.1 copy-start.6
  95.7 0.8 copy-start.5
  114.6 1.1 copy-start.6
  115.8 0.8 copy-start.5
  140.3 1.1 copy-start.6
  142.7 4.1 %copy-start.3 = (bf16[128,16,128]{0,2,1:T(8,128)(2,1)S(1)}, bf16[128,16,128]{0,2,1:T(8,128)(2,1)}, u32[]{:S(2)}) copy-start(bf16[128,16,128]{0,2,1:T(8,128)(2,1)} %copy-done.2) | copy-start | bytes 1572868
  146.8 1.2 copy-start.1
  151.6 12.5 %all-to-all-start.4 = ((bf16[16,2,8192]{2,1,0:T(2,128)(2,1)}), bf16[16,2,8192]{2,1,0:T(2,128)(2,1)S(1)}, u32[]{:S(2)}, u32[]{:S(2)}) async-start(bf16[16,2,8192]{2,1,0:T(2,128)(2,1)} %reshape.576), calls=%async_computation.4 | async-start | bytes 1048576 | tf_op jit(solution)/shard_map/all_to_all | solution.py:178
  164.1 14.6 %all-to-all-start.5 = ((bf16[16,2,8192]{2,1,0:T(2,128)(2,1)}), bf16[16,2,8192]{2,1,0:T(2,128)(2,1)S(1)}, u32[]{:S(2)}, u32[]{:S(2)}) async-start(bf16[16,2,8192]{2,1,0:T(2,128)(2,1)} %reshape.578), calls=%async_computation.5 | async-start | bytes 1048576 | tf_op jit(solution)/shard_map/all_to_all | solution.py:181
  178.7 128.1 %all-to-all-start.6 = ((bf16[16,2,8192]{2,1,0:T(2,128)(2,1)}), bf16[16,2,8192]{2,1,0:T(2,128)(2,1)S(1)}, u32[]{:S(2)}, u32[]{:S(2)}) async-start(bf16[16,2,8192]{2,1,0:T(2,128)(2,1)} %reshape.580), calls=%async_computation.6 | async-start | bytes 1048576 | tf_op jit(solution)/shard_map/all_to_all | solution.py:184
where the time goes:
time: 310 us; the launch traced here: 308 us
  blocking collectives  139 us (45%)
  matrix products  53.1 us (17%)
  waiting for transfers between devices  34.4 us (11%)
  local copies, waits for them, and re-layouts  30.6 us (10%)
  starting transfers between devices  30.2 us (10%)
  other arithmetic  19 us (6%)
    psum x1, blocking collectives, body(): gain_totals = lax.psum((query_gain_part, key_gain_part), ('dp', 'seq'))  121 us
    dot_general x20, matrix products, key_scores(): lax.dot_general(query_rows, key_rows, contract_last, preferred_element_ty...  27.3 us
    all_gather x1, blocking collectives, body(): segments = lax.all_gather(segment_ids, 'seq', axis=1, tiled=True)[0]  17.6 us
    unnamed x40, local copies, waits for them, and re-layouts  14.1 us
    dot_general x10, matrix products, backward_step(): jnp.dot(score_grads, key_rows, preferred_element_type=jnp.float32)  12.8 us
    all_to_all x1, waiting for transfers between devices, body(): lax.all_to_all(key_input.astype(jnp.bfloat16), 'seq', split_axis=0, conca...  8.96 us
    all_to_all x1, starting transfers between devices, body(): lax.all_to_all(q_pre[0], 'seq', split_axis=1, concat_axis=0, tiled=True)  7.72 us
    all_to_all x1, waiting for transfers between devices, body(): lax.all_to_all(value_copies, 'seq', split_axis=1, concat_axis=0, tiled=True)  6.98 us
  transfers between devices with their start and end apart: 7, of which 5 were waited for; matrix products, arithmetic and copies ran while one was open for 5% of the time, Pallas kernels for 0%

commit v1 on v0

--- a/solution.py
+++ b/solution.py
@@ -141,7 +141,9 @@
 
 
 def body(q_pre, k_pre, values, grad_out, segment_ids, q_gain, k_gain):
-    segments = lax.all_gather(segment_ids, "seq", axis=1, tiled=True)[0]
+    segments = jnp.concatenate(
+        lax.all_to_all(jnp.stack([segment_ids] * lax.axis_size("seq")), "seq", 0, 0), axis=1
+    )[0]
     positions, first = document_positions(segments, DOCS)
     local = q_pre.shape[1]
     heads = q_pre.shape[2]

time: 310 us -> 305 us (0.984)
  blocking collectives: 139 us -> 117 us
  waiting for transfers between devices: 34.4 us -> 41 us
  starting transfers between devices: 30.2 us -> 34.1 us
  other arithmetic: 19 us -> 22.9 us
    all_gather x1 -> x0, blocking collectives: 17.6 us -> none  [body(): segments = lax.all_gather(segment_ids, 'seq', axis=1, tiled=True)[0]]
    all_to_all x1, waiting for transfers between devices: 0.01 us -> 8.56 us  [body(): lax.all_to_all(q_pre[0], 'seq', split_axis=1, concat_axis=0, tiled=True)]
    all_to_all x0 -> x1, starting transfers between devices: none -> 7.58 us  [body(): lax.all_to_all(jnp.stack([segment_ids] * lax.axis_size('seq')), 'seq', 0, 0)]
    psum x1, blocking collectives: 121 us -> 117 us  [body(): gain_totals = lax.psum((query_gain_part, key_gain_part), ('dp', 'seq'))]
    all_to_all x1, starting transfers between devices: 7.72 us -> 4.43 us  [body(): lax.all_to_all(q_pre[0], 'seq', split_axis=1, concat_axis=0, tiled=True)]
    unnamed x40 -> x44, local copies, waits for them, and re-layouts: 14.1 us -> 12.9 us
  transfers between devices with their start and end apart: 7 -> 8, of which waited for: 5 -> 7; matrix products, arithmetic and copies ran while one was open for 5% -> 7% of each run, Pallas kernels for 0% -> 0%
where the time goes in v1:
time: 305 us; the launch traced here: 302 us
  blocking collectives  117 us (38%)
  matrix products  53.1 us (17%)
  waiting for transfers between devices  41 us (13%)
  starting transfers between devices  34.1 us (11%)
  local copies, waits for them, and re-layouts  32.1 us (11%)
  other arithmetic  22.9 us (8%)
    psum x1, blocking collectives, body(): gain_totals = lax.psum((query_gain_part, key_gain_part), ('dp', 'seq'))  117 us
    dot_general x20, matrix products, key_scores(): lax.dot_general(query_rows, key_rows, contract_last, preferred_element_ty...  27.3 us
    unnamed x44, local copies, waits for them, and re-layouts  12.9 us
    dot_general x10, matrix products, backward_step(): jnp.dot(score_grads, key_rows, preferred_element_type=jnp.float32)  12.8 us
    all_to_all x1, waiting for transfers between devices, body(): lax.all_to_all(q_pre[0], 'seq', split_axis=1, concat_axis=0, tiled=True)  8.56 us
    all_to_all x1, starting transfers between devices, body(): lax.all_to_all(jnp.stack([segment_ids] * lax.axis_size('seq')), 'seq', 0, 0)  7.58 us
    all_to_all x1, waiting for transfers between devices, body(): lax.all_to_all(value_copies, 'seq', split_axis=1, concat_axis=0, tiled=True)  7.03 us
    all_to_all x1, waiting for transfers between devices, body(): lax.all_to_all(key_input.astype(jnp.bfloat16), 'seq', split_axis=0, conca...  6.93 us
  transfers between devices with their start and end apart: 8, of which 7 were waited for; matrix products, arithmetic and copies ran while one was open for 7% of the time, Pallas kernels for 0%

profile of v1, /device:TPU:1, one launch (start us, length us, event | category | flops | bytes accessed | tf_op | source)
XLA Modules:
  0.0 302.5 jit_solution(2113326433874825028)
XLA Ops:
  1.9 7.6 %all-to-all-start.1 = ((s32[16,1,128]{2,1,0:T(1,128)}), s32[16,1,128]{2,1,0:T(1,128)S(1)}, u32[]{:S(2)}, u32[]{:S(2)}) async-start(s32[16,1,128]{2,1,0:T(1,128)} %stack.4), calls=%async_computation.1 | async-start | bytes 16384 | tf_op jit(solution)/shard_map/all_to_all | solution.py:145
  13.6 2.2 all-to-all-done.1
  15.8 4.4 %all-to-all-start = ((bf16[128,16,128]{2,0,1:T(8,128)(2,1)}), bf16[128,16,128]{2,0,1:T(8,128)(2,1)S(1)}, u32[]{:S(2)}, u32[]{:S(2)}) async-start(bf16[128,16,128]{2,0,1:T(8,128)(2,1)} %bitcast.131), calls=%async_computation | async-start | bytes 1048576 | tf_op jit(solution)/shard_map/all_to_all | solution.py:160
  20.7 8.6 %all-to-all-done = bf16[128,16,128]{2,0,1:T(8,128)(2,1)S(1)} async-done(((bf16[128,16,128]{2,0,1:T(8,128)(2,1)}), bf16[128,16,128]{2,0,1:T(8,128)(2,1)S(1)}, u32[]{:S(2)}, u32[]{:S(2)}) %all-to-all-start) | async-done | bytes 524320 | tf_op jit(solution)/shard_map/all_to_all | solution.py:160
  30.1 3.6 %all-to-all-start.2 = ((bf16[128,16,128]{0,2,1:T(8,128)(2,1)}), bf16[128,16,128]{0,2,1:T(8,128)(2,1)S(1)}, u32[]{:S(2)}, u32[]{:S(2)}) async-start(bf16[128,16,128]{0,2,1:T(8,128)(2,1)} %bitcast.13), calls=%async_computation.2 | async-start | bytes 1048576 | tf_op jit(solution)/shard_map/all_to_all | solution.py:162
  35.2 1.6 copy.145
  38.1 4.7 %all-to-all-done.2 = bf16[128,16,128]{0,2,1:T(8,128)(2,1)S(1)} async-done(((bf16[128,16,128]{0,2,1:T(8,128)(2,1)}), bf16[128,16,128]{0,2,1:T(8,128)(2,1)S(1)}, u32[]{:S(2)}, u32[]{:S(2)}) %all-to-all-start.2) | async-done | bytes 524320 | tf_op jit(solution)/shard_map/all_to_all | solution.py:162
  43.7 3.6 %all-to-all-start.3 = ((bf16[128,16,128]{2,0,1:T(8,128)(2,1)}), bf16[128,16,128]{2,0,1:T(8,128)(2,1)S(1)}, u32[]{:S(2)}, u32[]{:S(2)}) async-start(bf16[128,16,128]{2,0,1:T(8,128)(2,1)} %bitcast.21), calls=%async_computation.3 | async-start | bytes 1048576 | tf_op jit(solution)/shard_map/all_to_all | solution.py:163
  49.2 7.0 %all-to-all-done.3 = bf16[128,16,128]{2,0,1:T(8,128)(2,1)S(1)} async-done(((bf16[128,16,128]{2,0,1:T(8,128)(2,1)}), bf16[128,16,128]{2,0,1:T(8,128)(2,1)S(1)}, u32[]{:S(2)}, u32[]{:S(2)}) %all-to-all-start.3) | async-done | bytes 524320 | tf_op jit(solution)/shard_map/all_to_all | solution.py:163
  56.3 4.2 %all-to-all-start.4 = ((bf16[128,16,128]{2,0,1:T(8,128)(2,1)}), bf16[128,16,128]{2,0,1:T(8,128)(2,1)}, u32[]{:S(2)}, u32[]{:S(2)}) async-start(bf16[128,16,128]{2,0,1:T(8,128)(2,1)} %bitcast.130), calls=%async_computation.4 | async-start | bytes 1048576 | tf_op jit(solution)/shard_map/all_to_all | solution.py:161
  60.5 3.1 %fusion.63 = (bf16[2048,64]{0,1:T(8,128)(2,1)S(1)}, bf16[2048,64]{0,1:T(8,128)(2,1)S(1)}, bf16[2048,1,64]{0,2,1:T(8,128)(2,1)}, bf16[2048,1,64]{0,2,1:T(8,128)(2,1)}) fusion(f32[2048,1,128]{0,2,1:T(8,128)S(1)} %copy-done.5, f32[64]{0:T(128)S(1)} %negate_power_fusion, f32[2048]{0:T(1024)S(1)} %convert_multiply_fusion.1, f32[2048,1,128]{0,2,1:T(8,128)S(1)} %copy-done.4), kind=kLoop, calls=%fused_computation.97 | loop fusion | flops 2228224 | bytes 3154176 | tf_op jit(solution)/shard_map/jvp()/concatenate | solution.py:33
  64.8 4.8 %all-to-all-done.4 = bf16[128,16,128]{2,0,1:T(8,128)(2,1)} async-done(((bf16[128,16,128]{2,0,1:T(8,128)(2,1)}), bf16[128,16,128]{2,0,1:T(8,128)(2,1)}, u32[]{:S(2)}, u32[]{:S(2)}) %all-to-all-start.4) | async-done | bytes 524320 | tf_op jit(solution)/shard_map/all_to_all | solution.py:161
  70.8 69.0 %while.79 = (s32[]{:T(128)}, f32[2048,128]{0,1:T(8,128)}, f32[2048,128]{1,0:T(8,128)S(1)}, f32[2048,128]{1,0:T(8,128)S(1)}, bf16[2048,1,128]{0,2,1:T(8,128)(2,1)...) while((s32[]{:T(128)}, f32[2048,128]{0,1:T(8,128)}, ...), condition=%wide.region_12.13_spmd, body=%wide.region_5.12_spmd.sunk | while | flops 475268608 | bytes 14478353 | solution.py:139
  71.6 1.9 while.80
  71.8 1.4 fusion.101
  74.7 3.7 %while.81 = (s32[]{:T(128)}, f32[512,128]{1,0:T(8,128)S(1)}, f32[2048,128]{1,0:T(8,128)S(1)}, f32[2048,128]{1,0:T(8,128)S(1)}, s32[]{:T(128)}, /*index=5*/s32[51...) while((s32[]{:T(128)}, f32[512,128]{1,0:T(8,128)S(1)}, ...), condition=%wide.region_11.11_spmd.clone, body=%wide.region_10.10_spmd.clone.sunk | while | flops 338887680 | bytes 5656819 | solution.py:125
  80.5 3.7 %while.80 = (s32[]{:T(128)}, f32[512]{0:T(512)S(1)}, f32[512,128]{1,0:T(8,128)S(1)}, s32[]{:T(128)}, s32[512]{0:T(512)S(1)}, /*index=5*/s32[2048]{0:T(1024)S(1)}...) while((s32[]{:T(128)}, f32[512]{0:T(512)S(1)}, ...), condition=%wide.region_8.8_spmd.clone, body=%wide.region_6.7_spmd.clone.sunk | while | flops 136119296 | bytes 1990855 | solution.py:82
  85.5 7.4 %while.81 = (s32[]{:T(128)}, f32[512,128]{1,0:T(8,128)S(1)}, f32[2048,128]{1,0:T(8,128)S(1)}, f32[2048,128]{1,0:T(8,128)S(1)}, s32[]{:T(128)}, /*index=5*/s32[51...) while((s32[]{:T(128)}, f32[512,128]{1,0:T(8,128)S(1)}, ...), condition=%wide.region_11.11_spmd.clone, body=%wide.region_10.10_spmd.clone.sunk | while | flops 338887680 | bytes 5656819 | solution.py:125
  95.0 5.6 %while.80 = (s32[]{:T(128)}, f32[512]{0:T(512)S(1)}, f32[512,128]{1,0:T(8,128)S(1)}, s32[]{:T(128)}, s32[512]{0:T(512)S(1)}, /*index=5*/s32[2048]{0:T(1024)S(1)}...) while((s32[]{:T(128)}, f32[512]{0:T(512)S(1)}, ...), condition=%wide.region_8.8_spmd.clone, body=%wide.region_6.7_spmd.clone.sunk | while | flops 136119296 | bytes 1990855 | solution.py:82
  95.1 1.4 fusion.101
  101.8 11.1 %while.81 = (s32[]{:T(128)}, f32[512,128]{1,0:T(8,128)S(1)}, f32[2048,128]{1,0:T(8,128)S(1)}, f32[2048,128]{1,0:T(8,128)S(1)}, s32[]{:T(128)}, /*index=5*/s32[51...) while((s32[]{:T(128)}, f32[512,128]{1,0:T(8,128)S(1)}, ...), condition=%wide.region_11.11_spmd.clone, body=%wide.region_10.10_spmd.clone.sunk | while | flops 338887680 | bytes 5656819 | solution.py:125
  115.0 7.5 %while.80 = (s32[]{:T(128)}, f32[512]{0:T(512)S(1)}, f32[512,128]{1,0:T(8,128)S(1)}, s32[]{:T(128)}, s32[512]{0:T(512)S(1)}, /*index=5*/s32[2048]{0:T(1024)S(1)}...) while((s32[]{:T(128)}, f32[512]{0:T(512)S(1)}, ...), condition=%wide.region_8.8_spmd.clone, body=%wide.region_6.7_spmd.clone.sunk | while | flops 136119296 | bytes 1990855 | solution.py:82
  115.2 1.4 fusion.101
  123.7 14.8 %while.81 = (s32[]{:T(128)}, f32[512,128]{1,0:T(8,128)S(1)}, f32[2048,128]{1,0:T(8,128)S(1)}, f32[2048,128]{1,0:T(8,128)S(1)}, s32[]{:T(128)}, /*index=5*/s32[51...) while((s32[]{:T(128)}, f32[512,128]{1,0:T(8,128)S(1)}, ...), condition=%wide.region_11.11_spmd.clone, body=%wide.region_10.10_spmd.clone.sunk | while | flops 338887680 | bytes 5656819 | solution.py:125
  141.2 4.1 %fusion.60 = (f32[2048,1,64]{0,2,1:T(8,128)S(1)}, f32[2048,1,64]{0,2,1:T(8,128)S(1)}, f32[2048,1,64]{0,2,1:T(8,128)S(1)}, f32[2048,1,64]{0,2,1:T(8,128)S(1)}) fusion(f32[2048,1,128]{0,2,1:T(8,128)} %bitcast.159, f32[64]{0:T(128)S(1)} %negate_power_fusion, f32[2048]{0:T(1024)S(1)} %convert_multiply_fusion.1, f32[2048,1,128]{0,2,1:T(8,128)} %bitcast.158), kind=kLoop, calls=%fused_computation.89 | loop fusion | flops 1966080 | bytes 4202752 | tf_op jit(solution)/shard_map/transpose(jvp())/add_any | solution.py:34
  148.6 2.0 reduce.14
  151.8 3.6 %all-to-all-start.5 = ((bf16[16,2,8192]{2,1,0:T(2,128)(2,1)}), bf16[16,2,8192]{2,1,0:T(2,128)(2,1)S(1)}, u32[]{:S(2)}, u32[]{:S(2)}) async-start(bf16[16,2,8192]{2,1,0:T(2,128)(2,1)} %reshape.579), calls=%async_computation.5 | async-start | bytes 1048576 | tf_op jit(solution)/shard_map/all_to_all | solution.py:180
  157.6 6.8 %all-to-all-done.5 = bf16[16,2,8192]{2,1,0:T(2,128)(2,1)S(1)} async-done(((bf16[16,2,8192]{2,1,0:T(2,128)(2,1)}), bf16[16,2,8192]{2,1,0:T(2,128)(2,1)S(1)}, u32[]{:S(2)}, u32[]{:S(2)}) %all-to-all-start.5) | async-done | bytes 524320 | tf_op jit(solution)/shard_map/all_to_all | solution.py:180
  164.3 3.6 %all-to-all-start.6 = ((bf16[16,2,8192]{2,1,0:T(2,128)(2,1)}), bf16[16,2,8192]{2,1,0:T(2,128)(2,1)S(1)}, u32[]{:S(2)}, u32[]{:S(2)}) async-start(bf16[16,2,8192]{2,1,0:T(2,128)(2,1)} %reshape.581), calls=%async_computation.6 | async-start | bytes 1048576 | tf_op jit(solution)/shard_map/all_to_all | solution.py:183
  169.9 6.9 %all-to-all-done.6 = bf16[16,2,8192]{2,1,0:T(2,128)(2,1)S(1)} async-done(((bf16[16,2,8192]{2,1,0:T(2,128)(2,1)}), bf16[16,2,8192]{2,1,0:T(2,128)(2,1)S(1)}, u32[]{:S(2)}, u32[]{:S(2)}) %all-to-all-start.6) | async-done | bytes 524320 | tf_op jit(solution)/shard_map/all_to_all | solution.py:183
  176.9 3.6 %all-to-all-start.7 = ((bf16[16,2,8192]{2,1,0:T(2,128)(2,1)}), bf16[16,2,8192]{2,1,0:T(2,128)(2,1)S(1)}, u32[]{:S(2)}, u32[]{:S(2)}) async-start(bf16[16,2,8192]{2,1,0:T(2,128)(2,1)} %reshape.583), calls=%async_computation.7 | async-start | bytes 1048576 | tf_op jit(solution)/shard_map/all_to_all | solution.py:186
  180.5 117.0 %all-reduce.4 = (f32[128]{0:T(128)}, f32[128]{0:T(128)}) all-reduce(f32[128]{0:T(128)S(1)} %get-tuple-element.430, f32[128]{0:T(128)S(1)} %get-tuple-element.428), channel_id=1, replica_groups=mesh['dp'=32,'seq'=16] {'dp','seq'}, use_global_device_ids=true, to_apply=%region_18.19 | all-reduce | flops 256 | bytes 2048 | tf_op jit(solution)/shard_map/psum | solution.py:195
  (254 shorter events, 93.2 us)
Async XLA Ops:
  0.6 0.7 copy-start.15
  0.6 10.0 %copy-start.10 = (bf16[1,128,16,128]{3,2,1,0:T(8,128)(2,1)S(1)}, bf16[1,128,16,128]{3,2,1,0:T(8,128)(2,1)}, u32[]{:S(2)}) copy-start(bf16[1,128,16,128]{3,2,1,0:T(8,128)(2,1)} %param.13) | copy-start | bytes 1572868
  1.9 13.9 %all-to-all-start.1 = ((s32[16,1,128]{2,1,0:T(1,128)}), s32[16,1,128]{2,1,0:T(1,128)S(1)}, u32[]{:S(2)}, u32[]{:S(2)}) async-start(s32[16,1,128]{2,1,0:T(1,128)} %stack.4), calls=%async_computation.1 | async-start | bytes 16384 | tf_op jit(solution)/shard_map/all_to_all | solution.py:145
  10.7 1.0 copy-start.12
  11.6 1.0 copy-start.11
  15.8 13.4 %all-to-all-start = ((bf16[128,16,128]{2,0,1:T(8,128)(2,1)}), bf16[128,16,128]{2,0,1:T(8,128)(2,1)S(1)}, u32[]{:S(2)}, u32[]{:S(2)}) async-start(bf16[128,16,128]{2,0,1:T(8,128)(2,1)} %bitcast.131), calls=%async_computation | async-start | bytes 1048576 | tf_op jit(solution)/shard_map/all_to_all | solution.py:160
  30.1 12.6 %all-to-all-start.2 = ((bf16[128,16,128]{0,2,1:T(8,128)(2,1)}), bf16[128,16,128]{0,2,1:T(8,128)(2,1)S(1)}, u32[]{:S(2)}, u32[]{:S(2)}) async-start(bf16[128,16,128]{0,2,1:T(8,128)(2,1)} %bitcast.13), calls=%async_computation.2 | async-start | bytes 1048576 | tf_op jit(solution)/shard_map/all_to_all | solution.py:162
  35.2 1.6 copy-start.14
  36.8 1.3 copy-start
  42.8 4.7 %copy-start.2 = (bf16[128,16,128]{0,2,1:T(8,128)(2,1)}, bf16[128,16,128]{0,2,1:T(8,128)(2,1)S(1)}, u32[]{:S(2)}) copy-start(bf16[128,16,128]{0,2,1:T(8,128)(2,1)S(1)} %all-to-all-done.2) | copy-start | bytes 1572868
  43.7 12.5 %all-to-all-start.3 = ((bf16[128,16,128]{2,0,1:T(8,128)(2,1)}), bf16[128,16,128]{2,0,1:T(8,128)(2,1)S(1)}, u32[]{:S(2)}, u32[]{:S(2)}) async-start(bf16[128,16,128]{2,0,1:T(8,128)(2,1)} %bitcast.21), calls=%async_computation.3 | async-start | bytes 1048576 | tf_op jit(solution)/shard_map/all_to_all | solution.py:163
  47.4 0.7 copy-start.13
  48.1 12.4 %copy-start.4 = (f32[2048,1,128]{0,2,1:T(8,128)S(1)}, f32[2048,1,128]{0,2,1:T(8,128)}, u32[]{:S(2)}) copy-start(f32[2048,1,128]{0,2,1:T(8,128)} %multiply_multiply_fusion) | copy-start | bytes 3145732
  49.2 11.3 %copy-start.5 = (f32[2048,1,128]{0,2,1:T(8,128)S(1)}, f32[2048,1,128]{0,2,1:T(8,128)}, u32[]{:S(2)}) copy-start(f32[2048,1,128]{0,2,1:T(8,128)} %fusion.33) | copy-start | bytes 3145732
  56.3 13.2 %all-to-all-start.4 = ((bf16[128,16,128]{2,0,1:T(8,128)(2,1)}), bf16[128,16,128]{2,0,1:T(8,128)(2,1)}, u32[]{:S(2)}, u32[]{:S(2)}) async-start(bf16[128,16,128]{2,0,1:T(8,128)(2,1)} %bitcast.130), calls=%async_computation.4 | async-start | bytes 1048576 | tf_op jit(solution)/shard_map/all_to_all | solution.py:161
  63.7 1.0 copy-start.8
  63.7 1.0 copy-start.9
  70.8 0.8 copy-start.6
  78.6 1.1 copy-start.7
  79.7 0.8 copy-start.6
  93.0 1.1 copy-start.7
  94.2 0.8 copy-start.6
  113.1 1.1 copy-start.7
  114.2 0.8 copy-start.6
  138.7 1.1 copy-start.7
  141.2 4.1 %copy-start.3 = (bf16[128,16,128]{0,2,1:T(8,128)(2,1)S(1)}, bf16[128,16,128]{0,2,1:T(8,128)(2,1)}, u32[]{:S(2)}) copy-start(bf16[128,16,128]{0,2,1:T(8,128)(2,1)} %copy-done.2) | copy-start | bytes 1572868
  145.2 1.2 copy-start.1
  151.8 12.5 %all-to-all-start.5 = ((bf16[16,2,8192]{2,1,0:T(2,128)(2,1)}), bf16[16,2,8192]{2,1,0:T(2,128)(2,1)S(1)}, u32[]{:S(2)}, u32[]{:S(2)}) async-start(bf16[16,2,8192]{2,1,0:T(2,128)(2,1)} %reshape.579), calls=%async_computation.5 | async-start | bytes 1048576 | tf_op jit(solution)/shard_map/all_to_all | solution.py:180
  164.3 12.5 %all-to-all-start.6 = ((bf16[16,2,8192]{2,1,0:T(2,128)(2,1)}), bf16[16,2,8192]{2,1,0:T(2,128)(2,1)S(1)}, u32[]{:S(2)}, u32[]{:S(2)}) async-start(bf16[16,2,8192]{2,1,0:T(2,128)(2,1)} %reshape.581), calls=%async_computation.6 | async-start | bytes 1048576 | tf_op jit(solution)/shard_map/all_to_all | solution.py:183
  176.9 124.0 %all-to-all-start.7 = ((bf16[16,2,8192]{2,1,0:T(2,128)(2,1)}), bf16[16,2,8192]{2,1,0:T(2,128)(2,1)S(1)}, u32[]{:S(2)}, u32[]{:S(2)}) async-start(bf16[16,2,8192]{2,1,0:T(2,128)(2,1)} %reshape.583), calls=%async_computation.7 | async-start | bytes 1048576 | tf_op jit(solution)/shard_map/all_to_all | solution.py:186
